TPU v7x, 32 devices: a whole 2x2x4 slice. The times are simulated.
32 devices in a mesh: wide: 8 (over y, x, core), blk: 4 (over z).
Axes of the slice: x: 2, y: 2, z: 4, core: 2. Of those that a mesh axis runs over, the one named last changes fastest.
Arguments:
- visual_features: bfloat16 [32768, 1152], P(('wide', 'blk')), may hold values from -0.1875 to 0.1875
- sentence_features: bfloat16 [1024, 1152], P(('wide', 'blk')), may hold values from -0.1875 to 0.1875
- true_partner_ids: int32 [32768], P(('wide', 'blk')), may hold values from 0 to 1023
- inverse_warmth: float32 [], replicated, may hold values from 90 to 110
- additive_adjust: float32 [], replicated, may hold values from -12 to -9
Outputs:
- grad_images: float32 [32768, 1152], P(('wide', 'blk'))
- grad_texts: float32 [1024, 1152], P(('wide', 'blk'))
Inputs may be any that keep to these rules, and one draw needn't show every extreme that they name: Image i is paired with text true_partner_ids[i]; a text may be paired with several images or none.
All inputs are finite; a program needn't handle non-finite values.
Results may differ from a plain program's by a relative error of at most 0.007.
Values may be sent and summed in bfloat16 or wider, within the bound.
No kernel may reach another device: no remote copies, remote signals or barrier semaphores. Data moves between devices by JAX's collectives and lax.ppermute only.
A program may use at most 64 MiB of HBM per device.

v0:
```python
import jax
import jax.numpy as jnp
from jax import lax
from jax.sharding import PartitionSpec as P


def remaining_factors(
    visual_features, tile_length, true_partner_ids, leading_offset, inverse_warmth, additive_adjust
):
    cosine_grid = lax.dot_general(
        visual_features, tile_length, (((1,), (1,)), ((), ())), preferred_element_type=jnp.float32
    )
    sigmoid_levels = inverse_warmth * cosine_grid + additive_adjust
    columns = leading_offset + lax.iota(jnp.int32, tile_length.shape[0])
    plus_minus_ones = jnp.where(true_partner_ids[:, None] == columns[None, :], 1.0, -1.0).astype(
        jnp.float32
    )
    return (
        -inverse_warmth * plus_minus_ones * jax.nn.sigmoid(-plus_minus_ones * sigmoid_levels)
    ).astype(jnp.bfloat16)


def both_grads(visual_features, tile_length, loss_grid_scaled):
    incoming_grad_part = jnp.dot(loss_grid_scaled, tile_length, preferred_element_type=jnp.float32)
    returned_grad_part = lax.dot_general(
        loss_grid_scaled,
        visual_features,
        (((0,), (0,)), ((), ())),
        preferred_element_type=jnp.float32,
    )
    return (incoming_grad_part, returned_grad_part)


def shards(visual_features, sentence_features, true_partner_ids, inverse_warmth, additive_adjust):
    width = visual_features.shape[1]
    everything = lax.all_gather(sentence_features, ("wide", "blk"), axis=0, tiled=True)
    total = everything.shape[0]
    block = min(total, 1024)
    count = total // block
    blocks = everything.reshape(count, block, width)

    def scan_step(grad_img, running_dot_sums):
        piece, leading_offset = running_dot_sums
        loss_grid_scaled = remaining_factors(
            visual_features,
            piece,
            true_partner_ids,
            leading_offset,
            inverse_warmth,
            additive_adjust,
        )
        incoming_grad_part, returned_grad_part = both_grads(
            visual_features, piece, loss_grid_scaled
        )
        return (grad_img + incoming_grad_part, returned_grad_part)

    firsts = lax.iota(jnp.int32, count) * block
    grad_images, grad_blocks = lax.scan(
        scan_step, jnp.zeros(visual_features.shape, jnp.float32), (blocks, firsts)
    )
    grad_texts = lax.psum_scatter(
        grad_blocks.reshape(total, width), ("wide", "blk"), scatter_dimension=0, tiled=True
    )
    return (grad_images, grad_texts)


def solution(mesh):
    return jax.shard_map(
        shards,
        mesh=mesh,
        in_specs=(P(("wide", "blk"), None), P(("wide", "blk"), None), P(("wide", "blk")), P(), P()),
        out_specs=(P(("wide", "blk"), None), P(("wide", "blk"), None)),
        check_vma=False,
    )
```

profile of v0, /device:TPU:0, one launch (start us, length us, event | category | flops | bytes accessed | tf_op | source)
XLA Modules:
  0.0 195.8 jit_solution(3945152771545359974)
XLA Ops:
  7.2 0.0 copy-start
  7.2 0.0 all-gather.2.cloned.1.call-start
  7.2 0.7 all-gather.2.cloned.1.call-update
  7.9 0.0 reduce-scatter.2.cloned.1.call-start
  9.3 61.3 %all-gather.2.cloned.1.call-done = bf16[1024,1152]{1,0:T(8,128)(2,1)} async-done(((bf16[32,1152]{1,0:T(8,128)(2,1)}), bf16[1024,1152]{1,0:T(8,128)(2,1)}) %all-gather.2.cloned.1.call-update) | async-done | bytes 2359312 | tf_op jit(solution)/shard_map/all_gather | solution.py:36
  70.6 0.0 copy-done
  70.6 5.9 %fusion.1 = bf16[1024,1024]{1,0:T(8,128)(2,1)S(1)} fusion(bf16[1024,1152]{1,0:T(8,128)(2,1)S(1)} %copy-done, bf16[1024,1152]{1,0:T(8,128)(2,1)} %all-gather.2.cloned.1.call-done, f32[]{:T(128)S(6)} %copy.8, f32[]{:T(128)S(6)} %copy.7, s32[1024]{0:T(1024)} %param.7, f32[]{:T(128)S(6)} %neg.12), kind=kOutput, calls=%fused_computation.3 | convolution fusion | flops 2428502016 | bytes 6819852 | tf_op jit(solution)/shard_map/while/body/eval_jaxpr/dot_general | solution.py:10
  76.5 0.0 copy-start.1
  76.5 1.4 copy-done.1
  77.9 4.6 %fusion.8 = f32[1024,1152]{1,0:T(8,128)} fusion(bf16[1024,1024]{1,0:T(8,128)(2,1)S(1)} %fusion.1, bf16[1024,1152]{1,0:T(8,128)(2,1)S(1)} %copy-done), kind=kOutput, calls=%fused_computation.11 | convolution fusion | flops 2415919104 | bytes 9175040 | tf_op jit(solution)/shard_map/while/body/eval_jaxpr/dot_general | solution.py:25
  82.5 0.0 reduce-scatter.2.cloned.1.call-update
  82.5 7.4 %fusion.7 = f32[1024,1152]{1,0:T(8,128)} fusion(bf16[1024,1024]{1,0:T(8,128)(2,1)} %copy-done.1, bf16[1024,1152]{1,0:T(8,128)(2,1)} %all-gather.2.cloned.1.call-done), kind=kOutput, calls=%fused_computation.10 | convolution fusion | flops 2415919104 | bytes 9175040 | tf_op jit(solution)/shard_map/while/body/eval_jaxpr/dot_general | solution.py:24
  89.9 99.1 %reduce-scatter.2.cloned.1.call-done = f32[32,1152]{1,0:T(8,128)} async-done(((f32[1024,1152]{1,0:T(8,128)}), f32[32,1152]{1,0:T(8,128)}) %reduce-scatter.2.cloned.1.call-update) | async-done | bytes 147472 | tf_op jit(solution)/shard_map/reduce_scatter | solution.py:61
Async XLA Ops:
  7.2 63.4 %copy-start = (bf16[1024,1152]{1,0:T(8,128)(2,1)S(1)}, bf16[1024,1152]{1,0:T(8,128)(2,1)}, u32[]{:S(2)}) copy-start(bf16[1024,1152]{1,0:T(8,128)(2,1)} %param.5) | copy-start | bytes 7077892
  7.2 63.4 %all-gather.2.cloned.1.call-start = ((), (), s32[]{:S(2)}) async-start(), calls=%async_computation.1 | async-start | bytes 2433024 | tf_op jit(solution)/shard_map/all_gather | solution.py:36
  7.9 181.0 %reduce-scatter.2.cloned.1.call-start = ((), (), s32[]{:S(2)}) async-start(), calls=%async_computation.2 | async-start | bytes 4866048 | tf_op jit(solution)/shard_map/reduce_scatter | solution.py:61
  76.5 1.4 copy-start.1
Sparse Core Ops, SparseCore 0:
  10.8 59.7 all-gather.1
  82.6 106.2 reduce-scatter.1
where the time goes:
time: 196 us
  waiting for transfers between devices  161 us (82%)
  matrix products  17.9 us (9%)
  between operations  15.4 us (8%)
    reduce_scatter x1, waiting for transfers between devices, shards(): lax.psum_scatter(grad_blocks.reshape(total, width), ('wide', 'blk'), scat...  99.1 us
    all_gather x1, waiting for transfers between devices, shards(): lax.all_gather(sentence_features, ('wide', 'blk'), axis=0, tiled=True)  61.3 us
    dot_general x1, matrix products, both_grads(): jnp.dot(loss_grid_scaled, tile_length, preferred_element_type=jnp.float32)  7.36 us
    dot_general x1, matrix products, remaining_factors(): lax.dot_general(visual_features, tile_length, (((1,), (1,)), ((), ())), p...  5.92 us
    dot_general x1, matrix products, both_grads(): lax.dot_general(loss_grid_scaled, visual_features, (((0,), (0,)), ((), ()...  4.57 us
  transfers between devices with their start and end apart: 2, of which 2 were waited for; matrix products, arithmetic and copies ran while one was open for 4% of the time, Pallas kernels for 0%

commit v1 on v0

v1 whole, which is shorter than its diff:
```python
import functools

import jax
import jax.numpy as jnp
import numpy as np
from jax import lax
from jax.experimental import pallas as pl
from jax.experimental.pallas import tpu as pltpu
from jax.sharding import PartitionSpec as P

F32, BF16 = jnp.float32, jnp.bfloat16
ROWS, LANES = (((0,), (0,)), ((), ())), (((1,), (1,)), ((), ()))


def weight_block(texts, images, columns, partners, scale, bias):
    scores = lax.dot_general(texts, images, LANES, preferred_element_type=F32)
    logits = scale * scores + bias
    paired = columns == partners
    margin = jnp.where(paired, logits, -logits)
    factor = jnp.where(paired, -scale, scale)
    return (factor / (1.0 + jnp.exp(margin))).astype(BF16)


def weights_kernel(
    half, scale_ref, bias_ref, own_ref, other_ref, own_ids, other_ids, columns_ref, near_ref, far_ref,
    own_w, other_w, near_out, far_out, texts, total,
):
    step = pl.program_id(0)
    rows = near_ref.shape[0]

    @pl.when(step == 0)
    def _():
        texts[:rows] = near_ref[...]
        texts[rows:] = far_ref[...]
        total[...] = jnp.zeros_like(total)

    def block(images_ref, ids_ref, w_ref):
        w = weight_block(
            texts[...], images_ref[...], columns_ref[...], ids_ref[...], scale_ref[0], bias_ref[0]
        )
        w_ref[...] = w
        total[...] += jnp.dot(w, images_ref[...], preferred_element_type=F32)

    @pl.when(step < half)
    def _():
        block(own_ref, own_ids, own_w)

    @pl.when(step >= half)
    def _():
        block(other_ref, other_ids, other_w)

    @pl.when(step == pl.num_programs(0) - 1)
    def _():
        near_out[...] = total[:rows].astype(near_out.dtype)
        far_out[...] = total[rows:].astype(far_out.dtype)


def weights_and_texts(scale, bias, images, ids, columns, near, far, near_type):
    count, width = images[0].shape
    rows = near.shape[0]
    block = min(count, 512)
    half = count // block
    first = lambda i: jnp.minimum(i, half - 1)
    second = lambda i: jnp.maximum(i - half, 0)
    smem = pl.BlockSpec(memory_space=pltpu.SMEM)
    whole = lambda shape: pl.BlockSpec(shape, lambda i: (0, 0))
    return pl.pallas_call(
        functools.partial(weights_kernel, half),
        grid=(2 * half,),
        in_specs=[
            smem,
            smem,
            pl.BlockSpec((block, width), lambda i: (first(i), 0)),
            pl.BlockSpec((block, width), lambda i: (second(i), 0)),
            pl.BlockSpec((1, block), lambda i: (0, first(i))),
            pl.BlockSpec((1, block), lambda i: (0, second(i))),
            whole((2 * rows, 1)),
            whole((rows, width)),
            whole((rows, width)),
        ],
        out_specs=[
            pl.BlockSpec((2 * rows, block), lambda i: (0, first(i))),
            pl.BlockSpec((2 * rows, block), lambda i: (0, second(i))),
            whole((rows, width)),
            whole((rows, width)),
        ],
        out_shape=[
            jax.ShapeDtypeStruct((2 * rows, count), BF16),
            jax.ShapeDtypeStruct((2 * rows, count), BF16),
            jax.ShapeDtypeStruct((rows, width), near_type),
            jax.ShapeDtypeStruct((rows, width), BF16),
        ],
        scratch_shapes=[pltpu.VMEM((2 * rows, width), BF16), pltpu.VMEM((2 * rows, width), F32)],
        cost_estimate=pl.CostEstimate(
            flops=16 * rows * count * width,
            transcendentals=4 * rows * count,
            bytes_accessed=4 * count * width + 16 * rows * count,
        ),
    )(scale, bias, *images, *ids, columns, near, far)


def images_kernel(pieces, *refs):
    weights, texts, out = refs[: len(pieces)], refs[len(pieces) : -1], refs[-1]
    total, at = None, 0
    for w, parts in zip(weights, pieces):
        row = 0
        for _ in range(parts):
            text = texts[at]
            at += 1
            rows = text.shape[0]
            term = lax.dot_general(
                w[row : row + rows, :], text[...], ROWS, preferred_element_type=F32
            )
            total = term if total is None else total + term
            row += rows
    out[...] = total


def image_grads(weights, texts):
    count, width = weights[0].shape[1], texts[0][0].shape[1]
    block = min(count, 256)
    flat = [piece for group in texts for piece in group]
    rows = sum(piece.shape[0] for piece in flat)
    return pl.pallas_call(
        functools.partial(images_kernel, [len(group) for group in texts]),
        grid=(count // block,),
        in_specs=[pl.BlockSpec((w.shape[0], block), lambda i: (0, i)) for w in weights]
        + [pl.BlockSpec(piece.shape, lambda i: (0, 0)) for piece in flat],
        out_specs=pl.BlockSpec((block, width), lambda i: (i, 0)),
        out_shape=jax.ShapeDtypeStruct((count, width), F32),
        cost_estimate=pl.CostEstimate(
            flops=2 * rows * count * width,
            transcendentals=0,
            bytes_accessed=2 * rows * count + 4 * count * width,
        ),
    )(*weights, *flat)


def shards(wide, blk, images, texts, ids, scale, bias):
    rows, width = texts.shape
    plane = wide // 2

    def swap(array, axis, size, mask):
        return lax.ppermute(array, axis, [(i, i ^ mask) for i in range(size)])

    pair = lambda array: swap(array, "wide", wide, 1)
    across = lambda array, mask: swap(array, "wide", wide, 2 * mask)
    along = lambda array, mask: swap(array, "blk", blk, mask)

    scale, bias = scale.reshape(1), bias.reshape(1)
    ids = ids.reshape(1, -1)
    lines = [texts] + [along(texts, mask) for mask in range(1, blk)]
    both_images = (images, pair(images))
    both_ids = (ids, pair(ids))
    line = jnp.concatenate(lines)

    masks, places = np.meshgrid(np.arange(plane), np.arange(blk), indexing="ij")
    owner = (lax.axis_index("wide") ^ (2 * masks)) * blk + (lax.axis_index("blk") ^ places)
    columns = (owner[:, :, None] * rows + np.arange(rows)).reshape(plane, blk * rows, 1)

    groups = [line] + [across(line, mask) for mask in range(1, plane)]
    weights, grads, ours, theirs, their_texts = [], [], [], [], []
    for at in range(0, plane, 2):
        own_w, other_w, near, far = weights_and_texts(
            scale, bias, both_images, both_ids, columns[at : at + 2].reshape(-1, 1),
            groups[at], groups[at + 1], F32 if at == 0 else BF16,
        )
        grads += [near, far]
        ours.append(own_w)
        theirs.append(pair(other_w))
        their_texts.append([pair(groups[at]), pair(groups[at + 1])])

    mine = grads[0]
    for mask in range(1, plane):
        mine = mine + across(grads[mask], mask).astype(F32)
    parts = mine.reshape(blk, rows, width)
    grad_texts = parts[0]
    for mask in range(1, blk):
        grad_texts = grad_texts + along(parts[mask].astype(BF16), mask).astype(F32)

    our_texts = [[groups[at], groups[at + 1]] for at in range(0, plane, 2)]
    grad_images = image_grads(ours + theirs, our_texts + their_texts)
    return grad_images, grad_texts


def solution(mesh):
    wide, blk = mesh.shape["wide"], mesh.shape["blk"]
    both = P(("wide", "blk"), None)
    return jax.shard_map(
        functools.partial(shards, wide, blk),
        mesh=mesh,
        in_specs=(both, both, P(("wide", "blk")), P(), P()),
        out_specs=(both, both),
        check_vma=False,
    )
```

time: 196 us -> 80.2 us (0.41)
  waiting for transfers between devices: 161 us -> 26.9 us
  Pallas kernels: 0 us -> 24.1 us
  starting transfers between devices: 0.08 us -> 18.9 us
  matrix products: 17.9 us -> 0 us
  between operations: 15.4 us -> 2.13 us
  local copies, waits for them, and re-layouts: 1.39 us -> 5.12 us
  other arithmetic: 0 us -> 2.67 us
    reduce_scatter x1 -> x0, waiting for transfers between devices: 99.1 us -> none  [shards(): lax.psum_scatter(grad_blocks.reshape(total, width), ('wide', 'blk'), scat...]
    all_gather x1 -> x0, waiting for transfers between devices: 61.3 us -> none  [shards(): lax.all_gather(sentence_features, ('wide', 'blk'), axis=0, tiled=True)]
    ppermute x0 -> x20, waiting for transfers between devices: none -> 26.9 us  [swap(): return lax.ppermute(array, axis, [(i, i ^ mask) for i in range(size)])]
    pallas_call x0 -> x3, Pallas kernels: none -> 24.1 us  [the longest x2 15.3 us: weights_and_texts(): pl.pallas_call(functools.partial(weights_kernel, half), grid=(2 * half,),...]
    ppermute x0 -> x20, starting transfers between devices: none -> 18.9 us  [swap(): return lax.ppermute(array, axis, [(i, i ^ mask) for i in range(size)])]
    dot_general x3 -> x0, matrix products: 17.9 us -> none  [the longest x1 7.36 us: both_grads(): jnp.dot(loss_grid_scaled, tile_length, preferred_element_type=jnp.float32)]
    unnamed x4 -> x37, local copies, waits for them, and re-layouts: 1.39 us -> 3.5 us
  transfers between devices with their start and end apart: 2 -> 20, of which waited for: 2 -> 9; matrix products, arithmetic and copies ran while one was open for 4% -> 7% of each run, Pallas kernels for 0% -> 19%
where the time goes in v1:
time: 80.2 us; the launch traced here: 79.8 us
  waiting for transfers between devices  26.9 us (34%)
  Pallas kernels  24.1 us (30%)
  starting transfers between devices  18.9 us (24%)
  local copies, waits for them, and re-layouts  5.12 us (6%)
  other arithmetic  2.67 us (3%)
  between operations  2.13 us (3%)
    ppermute x20, waiting for transfers between devices, swap(): return lax.ppermute(array, axis, [(i, i ^ mask) for i in range(size)])  26.9 us
    ppermute x20, starting transfers between devices, swap(): return lax.ppermute(array, axis, [(i, i ^ mask) for i in range(size)])  18.9 us
    pallas_call x2, Pallas kernels, weights_and_texts(): pl.pallas_call(functools.partial(weights_kernel, half), grid=(2 * half,),...  15.3 us
    pallas_call x1, Pallas kernels, image_grads(): pl.pallas_call(functools.partial(images_kernel, [len(group) for group in...  8.75 us
    unnamed x37, local copies, waits for them, and re-layouts  3.5 us
  transfers between devices with their start and end apart: 20, of which 9 were waited for; matrix products, arithmetic and copies ran while one was open for 7% of the time, Pallas kernels for 19%

profile of v1, /device:TPU:0, one launch (start us, length us, event | category | flops | bytes accessed | tf_op | source)
XLA Modules:
  0.0 79.8 jit_solution(17829863192784121891)
XLA Ops:
  0.6 0.6 collective-permute-start
  1.2 3.7 %collective-permute-start.3 = (bf16[32,1152]{1,0:T(8,128)(2,1)}, bf16[32,1152]{1,0:T(8,128)(2,1)S(1)}, u32[]{:S(2)}, u32[]{:S(2)}) collective-permute-start(bf16[32,1152]{1,0:T(8,128)(2,1)} %param.9), channel_id=1, source_target_pairs={{0,2},{1,3},{2,0},{3,1},{4,6},{5,7},{6,4},{7,5},{8,10},{9,11},{10,... | collective-permute-start | bytes 221192 | tf_op jit(solution)/shard_map/ppermute | solution.py:144
  4.8 1.6 %collective-permute-start.2 = (bf16[32,1152]{1,0:T(8,128)(2,1)}, bf16[32,1152]{1,0:T(8,128)(2,1)S(1)}, u32[]{:S(2)}, u32[]{:S(2)}) collective-permute-start(bf16[32,1152]{1,0:T(8,128)(2,1)} %param.9), channel_id=1, source_target_pairs={{0,1},{1,0},{2,3},{3,2},{4,5},{5,4},{6,7},{7,6},{8,9},{9,8},{10,11... | collective-permute-start | bytes 221192 | tf_op jit(solution)/shard_map/ppermute | solution.py:144
  6.4 0.0 collective-permute-start.4
  6.4 0.0 collective-permute-start.1
  6.4 1.0 %constant_dynamic-update-slice_fusion.3 = bf16[128,1152]{1,0:T(8,128)(2,1)S(1)} fusion(bf16[32,1152]{1,0:T(8,128)(2,1)} %param.9), kind=kLoop, calls=%fused_computation.7 | loop fusion | bytes 147456
  7.4 0.7 add_multiply_fusion
  8.1 1.7 %collective-permute-done.2 = bf16[32,1152]{1,0:T(8,128)(2,1)S(1)} collective-permute-done((bf16[32,1152]{1,0:T(8,128)(2,1)}, bf16[32,1152]{1,0:T(8,128)(2,1)S(1)}, u32[]{:S(2)}, u32[]{:S(2)}) %collective-permute-start.2) | collective-permute-done | bytes 73760 | tf_op jit(solution)/shard_map/ppermute | solution.py:144
  9.8 0.0 collective-permute-done.3
  9.8 2.9 %collective-permute-done.4 = bf16[32,1152]{1,0:T(8,128)(2,1)S(1)} collective-permute-done((bf16[32,1152]{1,0:T(8,128)(2,1)}, bf16[32,1152]{1,0:T(8,128)(2,1)S(1)}, u32[]{:S(2)}, u32[]{:S(2)}) %collective-permute-start.4) | collective-permute-done | bytes 73760 | tf_op jit(solution)/shard_map/ppermute | solution.py:144
  12.8 2.5 %collective-permute-start.7 = (bf16[128,1152]{1,0:T(8,128)(2,1)S(1)}, bf16[128,1152]{1,0:T(8,128)(2,1)S(1)}, u32[]{:S(2)}, u32[]{:S(2)}) collective-permute-start(bf16[128,1152]{1,0:T(8,128)(2,1)S(1)} %constant_dynamic-update-slice_fusion.near_ref.refs_4_), channel_id=1, source_target_pairs={{0,24},{4,28},{8,16},{12,20},{16,8},{20,12},{24,0},{28,4},{1,25},{... | collective-permute-start | bytes 884744 | tf_op jit(solution)/shard_map/ppermute | solution.py:144
  15.3 0.5 collective-permute-start.6
  15.8 0.1 iota_add_fusion
  15.9 0.5 collective-permute-start.5
  17.7 0.8 reshape.42.columns_ref
  18.5 0.8 reshape.41.columns_ref
  19.3 0.0 collective-permute-done.1.other_ids
  19.3 4.4 %collective-permute-done.7.far_ref.refs_7_ = bf16[128,1152]{1,0:T(8,128)(2,1)S(1)} collective-permute-done((bf16[128,1152]{1,0:T(8,128)(2,1)S(1)}, bf16[128,1152]{1,0:T(8,128)(2,1)S(1)}, u32[]{:S(2)}, u32[]{:S(2)}) %collective-permute-start.7) | collective-permute-done | bytes 294944 | tf_op jit(solution)/shard_map/ppermute | solution.py:144
  23.7 4.1 %collective-permute-done.6.near_ref.refs_6_ = bf16[128,1152]{1,0:T(8,128)(2,1)S(1)} collective-permute-done((bf16[128,1152]{1,0:T(8,128)(2,1)S(1)}, bf16[128,1152]{1,0:T(8,128)(2,1)S(1)}, u32[]{:S(2)}, u32[]{:S(2)}) %collective-permute-start.6) | collective-permute-done | bytes 294944 | tf_op jit(solution)/shard_map/ppermute | solution.py:144
  27.8 0.0 collective-permute-done.other_ref
  27.8 0.0 copy-done.16
  27.8 0.0 copy-done.4
  27.8 0.7 copy-done.6
  28.5 7.6 %shard_map.96 = (bf16[256,1024]{1,0:T(8,128)(2,1)}, bf16[256,1024]{1,0:T(8,128)(2,1)}, bf16[128,1152]{1,0:T(8,128)(2,1)}, bf16[128,1152]{1,0:T(8,128)(2,1)}) custom-call(f32[1]{0:T(128)} %bitcast.4.scale_ref, f32[1]{0:T(128)} %bitcast.6.bias_ref, bf16[1024,1152]{1,0:T(8,128)(2,1)} %own_ref.3, bf16[1024,1152]{1,0:T(8,128)(2,1)} %collective-permute-done.other_ref, ...), custom_call_target="tpu_custom_call" | custom-call | flops 2415919104 | bytes 6815744 | tf_op jit(solution)/shard_map/pallas_call | solution.py:67
  36.1 0.0 copy-done.2
  36.2 1.6 %collective-permute-start.15 = (bf16[128,1152]{1,0:T(8,128)(2,1)}, bf16[128,1152]{1,0:T(8,128)(2,1)S(1)}, u32[]{:S(2)}, u32[]{:S(2)}) collective-permute-start(bf16[128,1152]{1,0:T(8,128)(2,1)} %get-tuple-element.16), channel_id=1, source_target_pairs={{0,16},{4,20},{8,24},{12,28},{16,0},{20,4},{24,8},{28,12},{1,17},{... | collective-permute-start | bytes 884744 | tf_op jit(solution)/shard_map/ppermute | solution.py:144
  37.7 1.4 %collective-permute-start.16 = (bf16[128,1152]{1,0:T(8,128)(2,1)}, bf16[128,1152]{1,0:T(8,128)(2,1)S(1)}, u32[]{:S(2)}, u32[]{:S(2)}) collective-permute-start(bf16[128,1152]{1,0:T(8,128)(2,1)} %get-tuple-element.17), channel_id=1, source_target_pairs={{0,24},{4,28},{8,16},{12,20},{16,8},{20,12},{24,0},{28,4},{1,25},{... | collective-permute-start | bytes 884744 | tf_op jit(solution)/shard_map/ppermute | solution.py:144
  39.2 0.0 collective-permute-done.5.far_ref.refs_5_
  39.2 0.7 copy-done.8
  39.9 7.7 %shard_map.95 = (bf16[256,1024]{1,0:T(8,128)(2,1)}, bf16[256,1024]{1,0:T(8,128)(2,1)}, f32[128,1152]{1,0:T(8,128)}, bf16[128,1152]{1,0:T(8,128)(2,1)}) custom-call(f32[1]{0:T(128)} %bitcast.3.scale_ref, f32[1]{0:T(128)} %bitcast.5.bias_ref, bf16[1024,1152]{1,0:T(8,128)(2,1)} %own_ref.3, bf16[1024,1152]{1,0:T(8,128)(2,1)} %collective-permute-done.other_ref, ...), custom_call_target="tpu_custom_call" | custom-call | flops 2415919104 | bytes 6815744 | tf_op jit(solution)/shard_map/pallas_call | solution.py:67
  47.7 0.0 copy-start.14
  47.7 0.0 copy-start.15
  47.7 0.6 collective-permute-start.14
  48.3 0.0 collective-permute-start.10
  48.3 3.4 %collective-permute-done.15 = bf16[128,1152]{1,0:T(8,128)(2,1)S(1)} collective-permute-done((bf16[128,1152]{1,0:T(8,128)(2,1)}, bf16[128,1152]{1,0:T(8,128)(2,1)S(1)}, u32[]{:S(2)}, u32[]{:S(2)}) %collective-permute-start.15) | collective-permute-done | bytes 294944 | tf_op jit(solution)/shard_map/ppermute | solution.py:144
  51.7 0.0 collective-permute-done.16
  51.7 4.7 %collective-permute-done.14 = bf16[128,1152]{1,0:T(8,128)(2,1)S(1)} collective-permute-done((bf16[128,1152]{1,0:T(8,128)(2,1)}, bf16[128,1152]{1,0:T(8,128)(2,1)S(1)}, u32[]{:S(2)}, u32[]{:S(2)}) %collective-permute-start.14) | collective-permute-done | bytes 294944 | tf_op jit(solution)/shard_map/ppermute | solution.py:144
  56.3 1.2 %fusion.2 = (bf16[128,1152]{1,0:T(8,128)(2,1)S(1)}, f32[128,1152]{1,0:T(8,128)S(1)}) fusion(bf16[128,1152]{1,0:T(8,128)(2,1)S(1)} %collective-permute-done.16, bf16[128,1152]{1,0:T(8,128)(2,1)S(1)} %collective-permute-done.15, f32[128,1152]{1,0:T(8,128)} %get-tuple-element.14, bf16[128,1152]{1,0:T(8,128)(2,1)S(1)} %collective-permute-done.14), kind=kLoop, calls=%fused_computation.10 | loop fusion | flops 1032192 | bytes 2359296 | tf_op jit(solution)/shard_map/convert.2
  57.6 2.0 %collective-permute-start.17 = (bf16[32,1152]{1,0:T(8,128)(2,1)S(1)}, bf16[32,1152]{1,0:T(8,128)(2,1)S(1)}, u32[]{:S(2)}, u32[]{:S(2)}) collective-permute-start(bf16[32,1152]{1,0:T(8,128)(2,1)S(1)} %get-tuple-element.20), channel_id=1, source_target_pairs={{0,1},{1,0},{2,3},{3,2},{4,5},{5,4},{6,7},{7,6},{8,9},{9,8},{10,11... | collective-permute-start | bytes 221192 | tf_op jit(solution)/shard_map/ppermute | solution.py:144
  59.6 3.3 %collective-permute-start.19 = (bf16[32,1152]{1,0:T(8,128)(2,1)S(1)}, bf16[32,1152]{1,0:T(8,128)(2,1)S(1)}, u32[]{:S(2)}, u32[]{:S(2)}) collective-permute-start(bf16[32,1152]{1,0:T(8,128)(2,1)S(1)} %get-tuple-element.21), channel_id=1, source_target_pairs={{0,3},{1,2},{2,1},{3,0},{4,7},{5,6},{6,5},{7,4},{8,11},{9,10},{10,... | collective-permute-start | bytes 221192 | tf_op jit(solution)/shard_map/ppermute | solution.py:144
  62.9 0.0 collective-permute-start.18
  62.9 0.0 collective-permute-start.9
  62.9 0.0 collective-permute-done.10.refs_8_
  62.9 0.0 copy-start.10
  62.9 0.0 copy-done.15
  62.9 0.5 collective-permute-start.8
  63.4 0.0 collective-permute-done.17
  63.4 0.1 collective-permute-start.13
  63.5 2.5 %collective-permute-done.19 = bf16[32,1152]{1,0:T(8,128)(2,1)S(1)} collective-permute-done((bf16[32,1152]{1,0:T(8,128)(2,1)S(1)}, bf16[32,1152]{1,0:T(8,128)(2,1)S(1)}, u32[]{:S(2)}, u32[]{:S(2)}) %collective-permute-start.19) | collective-permute-done | bytes 73760 | tf_op jit(solution)/shard_map/ppermute | solution.py:144
  66.1 0.0 copy-done.7
  66.1 0.0 collective-permute-start.12
  66.1 2.3 %collective-permute-done.18 = bf16[32,1152]{1,0:T(8,128)(2,1)S(1)} collective-permute-done((bf16[32,1152]{1,0:T(8,128)(2,1)S(1)}, bf16[32,1152]{1,0:T(8,128)(2,1)S(1)}, u32[]{:S(2)}, u32[]{:S(2)}) %collective-permute-start.18) | collective-permute-done | bytes 73760 | tf_op jit(solution)/shard_map/ppermute | solution.py:144
  68.3 0.0 collective-permute-start.11
  68.3 0.7 fusion.1
  69.0 0.0 collective-permute-done.13.refs_11_
  69.0 0.0 collective-permute-done.12.refs_10_
  69.1 0.0 copy-start.12
  69.1 0.9 %collective-permute-done.11.refs_9_ = bf16[128,1152]{1,0:T(8,128)(2,1)S(1)} collective-permute-done((bf16[128,1152]{1,0:T(8,128)(2,1)S(1)}, bf16[128,1152]{1,0:T(8,128)(2,1)S(1)}, u32[]{:S(2)}, u32[]{:S(2)}) %collective-permute-start.11) | collective-permute-done | bytes 294944 | tf_op jit(solution)/shard_map/ppermute | solution.py:144
  69.9 0.0 collective-permute-done.9.refs_3_
  69.9 0.0 collective-permute-done.8.refs_2_
  70.0 0.7 copy-done.13
  70.6 0.2 copy-done
  70.9 0.2 copy-done.1
  71.0 8.7 %shard_map.97 = f32[1024,1152]{1,0:T(8,128)} custom-call(bf16[256,1024]{1,0:T(8,128)(2,1)} %get-tuple-element.10.refs_0_, bf16[256,1024]{1,0:T(8,128)(2,1)} %get-tuple-element.11.refs_1_, bf16[256,1024]{1,0:T(8,128)(2,1)} %copy-done.1, bf16[256,1024]{1,0:T(8,128)(2,1)} %copy-done, bf16[128,1152]{1,0:T(8,128)(2,1)} %copy-done.2, bf16[128,1152]{1,0:T(8,128)(2,1)} %copy-done.8, ...), custom_call_target="tpu_custom_call" | custom-call | flops 2415919104 | bytes 6815744 | tf_op jit(solution)/shard_map/pallas_call | solution.py:124
  (25 shorter events, 0.1 us)
Async XLA Ops:
  0.6 27.2 %collective-permute-start = (bf16[1024,1152]{1,0:T(8,128)(2,1)}, bf16[1024,1152]{1,0:T(8,128)(2,1)}, u32[]{:S(2)}, u32[]{:S(2)}) collective-permute-start(bf16[1024,1152]{1,0:T(8,128)(2,1)} %own_ref.3), channel_id=1, source_target_pairs={{0,4},{4,0},{8,12},{12,8},{16,20},{20,16},{24,28},{28,24},{1,5},{5... | collective-permute-start | bytes 7077896 | tf_op jit(solution)/shard_map/ppermute | solution.py:144
  1.2 8.6 %collective-permute-start.3 = (bf16[32,1152]{1,0:T(8,128)(2,1)}, bf16[32,1152]{1,0:T(8,128)(2,1)S(1)}, u32[]{:S(2)}, u32[]{:S(2)}) collective-permute-start(bf16[32,1152]{1,0:T(8,128)(2,1)} %param.9), channel_id=1, source_target_pairs={{0,2},{1,3},{2,0},{3,1},{4,6},{5,7},{6,4},{7,5},{8,10},{9,11},{10,... | collective-permute-start | bytes 221192 | tf_op jit(solution)/shard_map/ppermute | solution.py:144
  4.8 5.0 %collective-permute-start.2 = (bf16[32,1152]{1,0:T(8,128)(2,1)}, bf16[32,1152]{1,0:T(8,128)(2,1)S(1)}, u32[]{:S(2)}, u32[]{:S(2)}) collective-permute-start(bf16[32,1152]{1,0:T(8,128)(2,1)} %param.9), channel_id=1, source_target_pairs={{0,1},{1,0},{2,3},{3,2},{4,5},{5,4},{6,7},{7,6},{8,9},{9,8},{10,11... | collective-permute-start | bytes 221192 | tf_op jit(solution)/shard_map/ppermute | solution.py:144
  6.4 6.4 %collective-permute-start.4 = (bf16[32,1152]{1,0:T(8,128)(2,1)}, bf16[32,1152]{1,0:T(8,128)(2,1)S(1)}, u32[]{:S(2)}, u32[]{:S(2)}) collective-permute-start(bf16[32,1152]{1,0:T(8,128)(2,1)} %param.9), channel_id=1, source_target_pairs={{0,3},{1,2},{2,1},{3,0},{4,7},{5,6},{6,5},{7,4},{8,11},{9,10},{10,... | collective-permute-start | bytes 221192 | tf_op jit(solution)/shard_map/ppermute | solution.py:144
  6.4 12.9 %collective-permute-start.1 = (s32[1,1024]{1,0:T(1,128)}, s32[1,1024]{1,0:T(1,128)S(1)}, u32[]{:S(2)}, u32[]{:S(2)}) collective-permute-start(s32[1,1024]{1,0:T(1,128)} %bitcast.7), channel_id=1, source_target_pairs={{0,4},{4,0},{8,12},{12,8},{16,20},{20,16},{24,28},{28,24},{1,5},{5... | collective-permute-start | bytes 12296 | tf_op jit(solution)/shard_map/ppermute | solution.py:144
  12.8 23.4 %copy-start.2 = (bf16[128,1152]{1,0:T(8,128)(2,1)}, bf16[128,1152]{1,0:T(8,128)(2,1)S(1)}, u32[]{:S(2)}) copy-start(bf16[128,1152]{1,0:T(8,128)(2,1)S(1)} %constant_dynamic-update-slice_fusion.near_ref.refs_4_) | copy-start | bytes 884740
  12.8 10.9 %collective-permute-start.7 = (bf16[128,1152]{1,0:T(8,128)(2,1)S(1)}, bf16[128,1152]{1,0:T(8,128)(2,1)S(1)}, u32[]{:S(2)}, u32[]{:S(2)}) collective-permute-start(bf16[128,1152]{1,0:T(8,128)(2,1)S(1)} %constant_dynamic-update-slice_fusion.near_ref.refs_4_), channel_id=1, source_target_pairs={{0,24},{4,28},{8,16},{12,20},{16,8},{20,12},{24,0},{28,4},{1,25},{... | collective-permute-start | bytes 884744 | tf_op jit(solution)/shard_map/ppermute | solution.py:144
  15.3 12.5 %collective-permute-start.6 = (bf16[128,1152]{1,0:T(8,128)(2,1)S(1)}, bf16[128,1152]{1,0:T(8,128)(2,1)S(1)}, u32[]{:S(2)}, u32[]{:S(2)}) collective-permute-start(bf16[128,1152]{1,0:T(8,128)(2,1)S(1)} %constant_dynamic-update-slice_fusion.near_ref.refs_4_), channel_id=1, source_target_pairs={{0,16},{4,20},{8,24},{12,28},{16,0},{20,4},{24,8},{28,12},{1,17},{... | collective-permute-start | bytes 884744 | tf_op jit(solution)/shard_map/ppermute | solution.py:144
  15.9 23.3 %collective-permute-start.5 = (bf16[128,1152]{1,0:T(8,128)(2,1)S(1)}, bf16[128,1152]{1,0:T(8,128)(2,1)S(1)}, u32[]{:S(2)}, u32[]{:S(2)}) collective-permute-start(bf16[128,1152]{1,0:T(8,128)(2,1)S(1)} %constant_dynamic-update-slice_fusion.near_ref.refs_4_), channel_id=1, source_target_pairs={{0,8},{4,12},{8,0},{12,4},{16,24},{20,28},{24,16},{28,20},{1,9},{5... | collective-permute-start | bytes 884744 | tf_op jit(solution)/shard_map/ppermute | solution.py:144
  19.3 8.5 %copy-start.16 = (s32[1,1024]{1,0:T(1,128)}, s32[1,1024]{1,0:T(1,128)S(1)}, u32[]{:S(2)}) copy-start(s32[1,1024]{1,0:T(1,128)S(1)} %collective-permute-done.1.other_ids) | copy-start | bytes 12292
  23.7 4.1 %copy-start.4 = (bf16[128,1152]{1,0:T(8,128)(2,1)}, bf16[128,1152]{1,0:T(8,128)(2,1)S(1)}, u32[]{:S(2)}) copy-start(bf16[128,1152]{1,0:T(8,128)(2,1)S(1)} %collective-permute-done.7.far_ref.refs_7_) | copy-start | bytes 884740
  27.8 0.7 copy-start.6
  36.2 15.5 %collective-permute-start.15 = (bf16[128,1152]{1,0:T(8,128)(2,1)}, bf16[128,1152]{1,0:T(8,128)(2,1)S(1)}, u32[]{:S(2)}, u32[]{:S(2)}) collective-permute-start(bf16[128,1152]{1,0:T(8,128)(2,1)} %get-tuple-element.16), channel_id=1, source_target_pairs={{0,16},{4,20},{8,24},{12,28},{16,0},{20,4},{24,8},{28,12},{1,17},{... | collective-permute-start | bytes 884744 | tf_op jit(solution)/shard_map/ppermute | solution.py:144
  37.7 13.9 %collective-permute-start.16 = (bf16[128,1152]{1,0:T(8,128)(2,1)}, bf16[128,1152]{1,0:T(8,128)(2,1)S(1)}, u32[]{:S(2)}, u32[]{:S(2)}) collective-permute-start(bf16[128,1152]{1,0:T(8,128)(2,1)} %get-tuple-element.17), channel_id=1, source_target_pairs={{0,24},{4,28},{8,16},{12,20},{16,8},{20,12},{24,0},{28,4},{1,25},{... | collective-permute-start | bytes 884744 | tf_op jit(solution)/shard_map/ppermute | solution.py:144
  39.2 0.7 copy-start.8
  39.9 8.4 %copy-start.3 = (bf16[128,1152]{1,0:T(8,128)(2,1)S(1)}, bf16[128,1152]{1,0:T(8,128)(2,1)}, u32[]{:S(2)}) copy-start(bf16[128,1152]{1,0:T(8,128)(2,1)} %copy-done.2) | copy-start | bytes 884740
  47.7 15.2 %copy-start.14 = (bf16[256,1024]{1,0:T(8,128)(2,1)S(1)}, bf16[256,1024]{1,0:T(8,128)(2,1)}, u32[]{:S(2)}) copy-start(bf16[256,1024]{1,0:T(8,128)(2,1)} %get-tuple-element.13) | copy-start | bytes 1572868
  47.7 15.2 %copy-start.15 = (bf16[256,1024]{1,0:T(8,128)(2,1)S(1)}, bf16[256,1024]{1,0:T(8,128)(2,1)}, u32[]{:S(2)}) copy-start(bf16[256,1024]{1,0:T(8,128)(2,1)} %get-tuple-element.12) | copy-start | bytes 1572868
  47.7 15.8 %copy-start.5 = (bf16[128,1152]{1,0:T(8,128)(2,1)S(1)}, bf16[128,1152]{1,0:T(8,128)(2,1)}, u32[]{:S(2)}) copy-start(bf16[128,1152]{1,0:T(8,128)(2,1)} %copy-done.4) | copy-start | bytes 884740
  47.7 18.4 %copy-start.7 = (bf16[128,1152]{1,0:T(8,128)(2,1)S(1)}, bf16[128,1152]{1,0:T(8,128)(2,1)}, u32[]{:S(2)}) copy-start(bf16[128,1152]{1,0:T(8,128)(2,1)} %copy-done.6) | copy-start | bytes 884740
  47.7 20.7 %copy-start.9 = (bf16[128,1152]{1,0:T(8,128)(2,1)S(1)}, bf16[128,1152]{1,0:T(8,128)(2,1)}, u32[]{:S(2)}) copy-start(bf16[128,1152]{1,0:T(8,128)(2,1)} %copy-done.8) | copy-start | bytes 884740
  47.7 8.6 %collective-permute-start.14 = (bf16[128,1152]{1,0:T(8,128)(2,1)}, bf16[128,1152]{1,0:T(8,128)(2,1)S(1)}, u32[]{:S(2)}, u32[]{:S(2)}) collective-permute-start(bf16[128,1152]{1,0:T(8,128)(2,1)} %get-tuple-element.15), channel_id=1, source_target_pairs={{0,8},{4,12},{8,0},{12,4},{16,24},{20,28},{24,16},{28,20},{1,9},{5... | collective-permute-start | bytes 884744 | tf_op jit(solution)/shard_map/ppermute | solution.py:144
  48.3 14.6 %collective-permute-start.10 = (bf16[128,1152]{1,0:T(8,128)(2,1)S(1)}, bf16[128,1152]{1,0:T(8,128)(2,1)S(1)}, u32[]{:S(2)}, u32[]{:S(2)}) collective-permute-start(bf16[128,1152]{1,0:T(8,128)(2,1)S(1)} %copy-done.3), channel_id=1, source_target_pairs={{0,4},{4,0},{8,12},{12,8},{16,20},{20,16},{24,28},{28,24},{1,5},{5... | collective-permute-start | bytes 884744 | tf_op jit(solution)/shard_map/ppermute | solution.py:144
  57.6 5.9 %collective-permute-start.17 = (bf16[32,1152]{1,0:T(8,128)(2,1)S(1)}, bf16[32,1152]{1,0:T(8,128)(2,1)S(1)}, u32[]{:S(2)}, u32[]{:S(2)}) collective-permute-start(bf16[32,1152]{1,0:T(8,128)(2,1)S(1)} %get-tuple-element.20), channel_id=1, source_target_pairs={{0,1},{1,0},{2,3},{3,2},{4,5},{5,4},{6,7},{7,6},{8,9},{9,8},{10,11... | collective-permute-start | bytes 221192 | tf_op jit(solution)/shard_map/ppermute | solution.py:144
  59.6 6.5 %collective-permute-start.19 = (bf16[32,1152]{1,0:T(8,128)(2,1)S(1)}, bf16[32,1152]{1,0:T(8,128)(2,1)S(1)}, u32[]{:S(2)}, u32[]{:S(2)}) collective-permute-start(bf16[32,1152]{1,0:T(8,128)(2,1)S(1)} %get-tuple-element.21), channel_id=1, source_target_pairs={{0,3},{1,2},{2,1},{3,0},{4,7},{5,6},{6,5},{7,4},{8,11},{9,10},{10,... | collective-permute-start | bytes 221192 | tf_op jit(solution)/shard_map/ppermute | solution.py:144
  62.9 5.5 %collective-permute-start.18 = (bf16[32,1152]{1,0:T(8,128)(2,1)S(1)}, bf16[32,1152]{1,0:T(8,128)(2,1)S(1)}, u32[]{:S(2)}, u32[]{:S(2)}) collective-permute-start(bf16[32,1152]{1,0:T(8,128)(2,1)S(1)} %get-tuple-element.22), channel_id=1, source_target_pairs={{0,2},{1,3},{2,0},{3,1},{4,6},{5,7},{6,4},{7,5},{8,10},{9,11},{10,... | collective-permute-start | bytes 221192 | tf_op jit(solution)/shard_map/ppermute | solution.py:144
  62.9 7.1 %collective-permute-start.9 = (bf16[256,1024]{1,0:T(8,128)(2,1)S(1)}, bf16[256,1024]{1,0:T(8,128)(2,1)S(1)}, u32[]{:S(2)}, u32[]{:S(2)}) collective-permute-start(bf16[256,1024]{1,0:T(8,128)(2,1)S(1)} %copy-done.14), channel_id=1, source_target_pairs={{0,4},{4,0},{8,12},{12,8},{16,20},{20,16},{24,28},{28,24},{1,5},{5... | collective-permute-start | bytes 1572872 | tf_op jit(solution)/shard_map/ppermute | solution.py:144
  62.9 7.1 %copy-start.10 = (bf16[128,1152]{1,0:T(8,128)(2,1)}, bf16[128,1152]{1,0:T(8,128)(2,1)S(1)}, u32[]{:S(2)}) copy-start(bf16[128,1152]{1,0:T(8,128)(2,1)S(1)} %collective-permute-done.10.refs_8_) | copy-start | bytes 884740
  62.9 7.0 %collective-permute-start.8 = (bf16[256,1024]{1,0:T(8,128)(2,1)S(1)}, bf16[256,1024]{1,0:T(8,128)(2,1)S(1)}, u32[]{:S(2)}, u32[]{:S(2)}) collective-permute-start(bf16[256,1024]{1,0:T(8,128)(2,1)S(1)} %copy-done.15), channel_id=1, source_target_pairs={{0,4},{4,0},{8,12},{12,8},{16,20},{20,16},{24,28},{28,24},{1,5},{5... | collective-permute-start | bytes 1572872 | tf_op jit(solution)/shard_map/ppermute | solution.py:144
  63.4 5.6 %collective-permute-start.13 = (bf16[128,1152]{1,0:T(8,128)(2,1)S(1)}, bf16[128,1152]{1,0:T(8,128)(2,1)S(1)}, u32[]{:S(2)}, u32[]{:S(2)}) collective-permute-start(bf16[128,1152]{1,0:T(8,128)(2,1)S(1)} %copy-done.5), channel_id=1, source_target_pairs={{0,4},{4,0},{8,12},{12,8},{16,20},{20,16},{24,28},{28,24},{1,5},{5... | collective-permute-start | bytes 884744 | tf_op jit(solution)/shard_map/ppermute | solution.py:144
  66.1 3.0 %collective-permute-start.12 = (bf16[128,1152]{1,0:T(8,128)(2,1)S(1)}, bf16[128,1152]{1,0:T(8,128)(2,1)S(1)}, u32[]{:S(2)}, u32[]{:S(2)}) collective-permute-start(bf16[128,1152]{1,0:T(8,128)(2,1)S(1)} %copy-done.7), channel_id=1, source_target_pairs={{0,4},{4,0},{8,12},{12,8},{16,20},{20,16},{24,28},{28,24},{1,5},{5... | collective-permute-start | bytes 884744 | tf_op jit(solution)/shard_map/ppermute | solution.py:144
  68.3 1.6 %collective-permute-start.11 = (bf16[128,1152]{1,0:T(8,128)(2,1)S(1)}, bf16[128,1152]{1,0:T(8,128)(2,1)S(1)}, u32[]{:S(2)}, u32[]{:S(2)}) collective-permute-start(bf16[128,1152]{1,0:T(8,128)(2,1)S(1)} %copy-done.9), channel_id=1, source_target_pairs={{0,4},{4,0},{8,12},{12,8},{16,20},{20,16},{24,28},{28,24},{1,5},{5... | collective-permute-start | bytes 884744 | tf_op jit(solution)/shard_map/ppermute | solution.py:144
  69.0 0.9 %copy-start.11 = (bf16[128,1152]{1,0:T(8,128)(2,1)}, bf16[128,1152]{1,0:T(8,128)(2,1)S(1)}, u32[]{:S(2)}) copy-start(bf16[128,1152]{1,0:T(8,128)(2,1)S(1)} %collective-permute-done.13.refs_11_) | copy-start | bytes 884740
  69.1 0.9 %copy-start.12 = (bf16[128,1152]{1,0:T(8,128)(2,1)}, bf16[128,1152]{1,0:T(8,128)(2,1)S(1)}, u32[]{:S(2)}) copy-start(bf16[128,1152]{1,0:T(8,128)(2,1)S(1)} %collective-permute-done.12.refs_10_) | copy-start | bytes 884740
  69.9 0.7 copy-start.13
  69.9 0.9 %copy-start = (bf16[256,1024]{1,0:T(8,128)(2,1)}, bf16[256,1024]{1,0:T(8,128)(2,1)S(1)}, u32[]{:S(2)}) copy-start(bf16[256,1024]{1,0:T(8,128)(2,1)S(1)} %collective-permute-done.9.refs_3_) | copy-start | bytes 1572868
  69.9 1.1 %copy-start.1 = (bf16[256,1024]{1,0:T(8,128)(2,1)}, bf16[256,1024]{1,0:T(8,128)(2,1)S(1)}, u32[]{:S(2)}) copy-start(bf16[256,1024]{1,0:T(8,128)(2,1)S(1)} %collective-permute-done.8.refs_2_) | copy-start | bytes 1572868
